TPU v7x, 256 devices: a whole 4x4x8 slice. The times are simulated.
256 devices in a mesh: seq: 32 (over z, y), grp: 8 (over x, core).
Axes of the slice: x: 4, y: 4, z: 8, core: 2. Of those that a mesh axis runs over, the one named last changes fastest.
Arguments:
- x_in: bfloat16 [4096, 8192], P('seq', 'grp'), may hold values from -6 to 6
- multiplier_channels: bfloat16 [4096, 8192], P('seq', 'grp'), may hold values from -6 to 6
- b_proj: bfloat16 [4096, 1024], P('seq', 'grp'), may hold values from -6 to 6
- c_proj: bfloat16 [4096, 1024], P('seq', 'grp'), may hold values from -0.5 to 0.5
- dt_raw: float32 [4096, 64], P('seq', 'grp'), as said below
- dt_bias: float32 [64], P('grp'), may hold values from -3.5 to -1.5
- a_log: float32 [64], P('grp'), as said below
- skip_d: float32 [64], P('grp'), may hold values from 0.2 to 1
- norm_gain: float32 [8192], P('grp'), may hold values from 0.5 to 1.5
- w_out: bfloat16 [8192, 8192], P('grp', 'seq'), may hold values from -0.03125 to 0.03125
Outputs:
- mixed: bfloat16 [4096, 8192], P('seq', 'grp')
Inputs may be any that keep to these rules, and one draw needn't show every extreme that they name: `dt_raw`: step size offsets, with bursts at a few positions of the sequence shared by all heads. `a_log`: log decay rates per head, between log(0.1 / (0.08 * 4096)) and log(0.6).
All inputs are finite; a program needn't handle non-finite values.
Results may differ from a plain program's by a relative error of at most 0.0049.
Values may be sent and summed in bfloat16 or wider, within the bound.
A program may use at most 128 MiB of HBM per device.

v0:
```python
import math
import jax
import jax.numpy as jnp
from jax import lax
from jax.sharding import PartitionSpec as P

CHANNEL_WIDTH = 128
STATE = 128
HIGH = lax.Precision.HIGHEST


def prefix(array, axis, combine, identity):
    length, mine = (lax.axis_size(axis), lax.axis_index(axis))
    everything = jax.tree.map(lambda part: lax.all_gather(part, axis), array)
    start = jax.tree.map(
        lambda part, zero: jnp.broadcast_to(jnp.asarray(zero, part.dtype), part.shape),
        array,
        identity,
    )

    def turn(k, before):
        reached = k < mine
        new = combine(before, jax.tree.map(lambda part: part[k], everything))
        return jax.tree.map(lambda a, b: jnp.where(reached, a, b), new, before)

    return lax.fori_loop(0, length, turn, start)


def ssd_blocks(xf, dt, la, bm, cm, braw, craw, init):
    length, heads, width = xf.shape
    groups = bm.shape[1]
    ratio = heads // groups
    block = math.gcd(length, 256)
    count = length // block

    def step(state, blk):
        xb, dtb, lab, bb, cb, bnar, cnar = blk
        cum = jnp.cumsum(lab, axis=0)
        attention_logits = jnp.einsum(
            "tgn,sgn->gts", cnar, bnar, preferred_element_type=jnp.float32
        )
        attention_logits = jnp.repeat(attention_logits, ratio, axis=0)
        diff = cum.T[:, :, None] - cum.T[:, None, :]
        rows = lax.broadcasted_iota(jnp.int32, (block, block), 0)
        cols = lax.broadcasted_iota(jnp.int32, (block, block), 1)
        mask = (rows >= cols)[None, :, :]
        decay = jnp.exp(jnp.where(mask, diff, -1e30))
        mixing = decay * attention_logits * dtb.T[:, None, :]
        outs = jnp.einsum("hts,shp->thp", mixing, xb, precision=HIGH)
        cheads = jnp.repeat(cb, ratio, axis=1)
        incoming_channel_bundles = jnp.repeat(bb, ratio, axis=1)
        outs = outs + jnp.exp(cum)[:, :, None] * jnp.einsum(
            "thn,hpn->thp", cheads, state, precision=HIGH
        )
        weights = jnp.exp(cum[-1][None, :] - cum) * dtb
        fresh = jnp.einsum("sh,shp,shn->hpn", weights, xb, incoming_channel_bundles, precision=HIGH)
        state = jnp.exp(cum[-1])[:, None, None] * state + fresh
        return (state, outs)

    blocks = (
        xf.reshape(count, block, heads, width),
        dt.reshape(count, block, heads),
        la.reshape(count, block, heads),
        bm.reshape(count, block, groups, -1),
        cm.reshape(count, block, groups, -1),
        braw.reshape(count, block, groups, -1),
        craw.reshape(count, block, groups, -1),
    )
    final, outs = lax.scan(step, init, blocks)
    return (outs.reshape(length, heads, width), final, jnp.sum(la, axis=0))


def gated_norm_output(y, multiplier_channels, norm_gain, groups):
    length = y.shape[0]
    gated = y.reshape(length, -1) * jax.nn.silu(multiplier_channels.astype(jnp.float32))
    split = gated.reshape(length, groups, -1)
    split = split * lax.rsqrt(jnp.mean(split * split, axis=-1, keepdims=True) + 1e-05)
    return (split.reshape(length, -1) * norm_gain).astype(jnp.bfloat16)


def combine_states(earlier_state, later):
    return (earlier_state[0] * later[0], later[0][:, None, None] * earlier_state[1] + later[1])


def shards(
    x_in, multiplier_channels, b_proj, c_proj, dt_raw, dt_bias, a_log, skip_d, norm_gain, w_out
):
    length = x_in.shape[0]
    heads = dt_raw.shape[1]
    groups = b_proj.shape[1] // STATE
    xf = x_in.astype(jnp.float32).reshape(length, heads, CHANNEL_WIDTH)
    dt = jax.nn.softplus(dt_raw + dt_bias)
    la = -jnp.exp(a_log) * dt
    braw = b_proj.reshape(length, groups, STATE)
    craw = c_proj.reshape(length, groups, STATE)
    bm = braw.astype(jnp.float32)
    cm = craw.astype(jnp.float32)
    empty = jnp.zeros((heads, CHANNEL_WIDTH, STATE), jnp.float32)
    y, local_end, total = ssd_blocks(xf, dt, la, bm, cm, braw, craw, empty)
    identity = (jnp.ones((heads,), jnp.float32), empty)
    carried = prefix((jnp.exp(total), local_end), "seq", combine_states, identity)
    cum = jnp.cumsum(la, axis=0)
    cheads = jnp.repeat(cm, heads // groups, axis=1)
    y = y + jnp.exp(cum)[:, :, None] * jnp.einsum(
        "thn,hpn->thp", cheads, carried[1], precision=HIGH
    )
    y = y + skip_d[None, :, None] * xf
    normed = gated_norm_output(y, multiplier_channels, norm_gain, groups)
    partial_out = jnp.dot(
        normed, lax.all_gather(w_out, "seq", axis=1, tiled=True), preferred_element_type=jnp.float32
    )
    return lax.psum_scatter(partial_out, "grp", scatter_dimension=1, tiled=True).astype(
        jnp.bfloat16
    )


def solution(mesh):
    return jax.shard_map(
        shards,
        mesh=mesh,
        in_specs=(
            P("seq", "grp"),
            P("seq", "grp"),
            P("seq", "grp"),
            P("seq", "grp"),
            P("seq", "grp"),
            P("grp"),
            P("grp"),
            P("grp"),
            P("grp"),
            P("grp", "seq"),
        ),
        out_specs=P("seq", "grp"),
        check_vma=False,
    )
```

profile of v0, /device:TPU:8, one launch (start us, length us, event | category | flops | bytes accessed | tf_op | source)
XLA Modules:
  0.0 363.0 jit_solution(16501429066232339684)
XLA Ops:
  6.5 0.0 all-gather.7.cloned.1.call-start
  6.5 0.7 exponential_negate_fusion
  7.2 0.9 fusion.33
  8.1 0.1 copy.35
  8.2 0.2 reduce_window_sum.13
  8.5 1.1 copy.38
  9.6 0.8 convert_element_type.19
  10.4 0.8 exponential_multiply_fusion
  11.2 1.4 convolution_add_fusion
  12.6 0.0 all-gather.7.cloned.1.call-update
  12.6 0.0 all-gather.5.cloned.1.call-start
  12.7 0.7 all-gather.5.cloned.1.call-update
  13.4 0.0 reduce-scatter.2.cloned.1.call-start
  13.5 0.1 copy.39
  13.6 0.8 convert_element_type.18
  14.4 1.3 dynamic-slice.6
  16.3 0.1 exponential_dynamic-update-slice_fusion
  16.4 74.4 %all-reduce = f32[256]{0:T(256)S(1)} all-reduce(f32[256]{0:T(256)S(1)} %exponential_dynamic-update-slice_fusion), channel_id=2, replica_groups=mesh['seq'=32,'grp'=8] {'seq'}, use_global_device_ids=true, to_apply=%add | all-reduce | flops 256 | bytes 2048
  90.8 0.1 reshape.106
  90.9 0.9 fusion.34
  91.8 0.8 convolution_bitcast_fusion
  92.6 1.2 fusion.5
  93.8 61.4 %all-gather.7.cloned.1.call-done = f32[256,128,128]{2,1,0:T(8,128)} async-done(((f32[8,128,128]{2,1,0:T(8,128)}), f32[256,128,128]{2,1,0:T(8,128)}) %all-gather.7.cloned.1.call-update) | async-done | bytes 16777232 | tf_op jit(solution)/shard_map/all_gather | solution.py:14
  155.2 39.0 %while.9 = (s32[]{:T(128)}, f32[8,128,128]{2,1,0:T(8,128)S(1)}, s32[]{:T(128)}, f32[32,8]{1,0:T(8,128)S(1)}, f32[32,8,128,128]{3,2,1,0:T(8,128)}, /*index=5*/s32[]{:T(128)}, s32[]{:T(128)}) while((s32[]{:T(128)}, f32[8,128,128]{2,1,0:T(8,128)S(1)}, s32[]{:T(128)}, f32[32,8]{1,0:T(8,128)S(1)}, f32[32,8,128,128]{3,2,1,0:T(8,128)}, ...), condition=%wide.region_3.4_spmd.clone, body=%wide.region_2.3_spmd.clone.sunk | while | flops 524292 | bytes 1573065 | solution.py:26
  155.2 1.2 fusion.41
  156.4 1.2 fusion.41
  157.6 1.2 fusion.41
  158.8 1.2 fusion.41
  160.1 1.2 fusion.41
  161.3 1.2 fusion.41
  162.5 1.2 fusion.41
  163.7 1.2 fusion.41
  164.9 1.2 fusion.41
  166.1 1.2 fusion.41
  167.3 1.2 fusion.41
  168.6 1.2 fusion.41
  169.8 1.2 fusion.41
  171.1 1.2 fusion.41
  172.3 1.2 fusion.41
  173.5 1.2 fusion.41
  174.7 1.2 fusion.41
  175.9 1.2 fusion.41
  177.2 1.2 fusion.41
  178.4 1.2 fusion.41
  179.6 1.2 fusion.41
  180.8 1.2 fusion.41
  182.0 1.2 fusion.41
  183.2 1.2 fusion.41
  184.5 1.2 fusion.41
  185.7 1.2 fusion.41
  186.9 1.2 fusion.41
  188.1 1.2 fusion.41
  189.3 1.2 fusion.41
  190.5 1.2 fusion.41
  191.8 1.2 fusion.41
  193.0 1.2 fusion.41
  194.2 1.9 fusion.3
  196.0 0.2 copy.41
  196.3 0.2 multiply_reduce_fusion
  196.5 108.9 %all-gather.5.cloned.1.call-done = bf16[1024,8192]{1,0:T(8,128)(2,1)} async-done(((bf16[1024,256]{1,0:T(8,128)(2,1)}), bf16[1024,8192]{1,0:T(8,128)(2,1)}) %all-gather.5.cloned.1.call-update) | async-done | bytes 16777232 | tf_op jit(solution)/shard_map/all_gather | solution.py:110
  305.4 10.2 %fusion.15 = f32[128,8192]{1,0:T(8,128)} fusion(bf16[1024,8192]{1,0:T(8,128)(2,1)} %all-gather.5.cloned.1.call-done, f32[1024]{0:T(1024)S(1)} %copy-done.1, f32[128]{0:T(128)S(1)} %add_rsqrt_fusion, f32[128,1024]{1,0:T(8,128)S(1)} %copy.41, bf16[128,1024]{1,0:T(8,128)(2,1)S(1)} %copy-done), kind=kOutput, calls=%fused_computation.27 | convolution fusion | flops 2148663296 | bytes 21762560 | tf_op jit(solution)/shard_map/dot_general | solution.py:109
  315.6 0.0 reduce-scatter.2.cloned.1.call-update
  315.6 39.0 %reduce-scatter.2.cloned.1.call-done = f32[128,1024]{1,0:T(8,128)} async-done(((f32[128,8192]{1,0:T(8,128)}), f32[128,1024]{1,0:T(8,128)}) %reduce-scatter.2.cloned.1.call-update) | async-done | bytes 524304 | tf_op jit(solution)/shard_map/reduce_scatter | solution.py:112
  354.7 1.8 convert_element_type.22
  (45 shorter events, 0.5 us)
Async XLA Ops:
  6.5 189.7 %copy-start = (bf16[128,1024]{1,0:T(8,128)(2,1)S(1)}, bf16[128,1024]{1,0:T(8,128)(2,1)}, u32[]{:S(2)}) copy-start(bf16[128,1024]{1,0:T(8,128)(2,1)} %param.13) | copy-start | bytes 786436
  6.5 298.9 %copy-start.1 = (f32[1024]{0:T(1024)S(1)}, f32[1024]{0:T(1024)}, u32[]{:S(2)}) copy-start(f32[1024]{0:T(1024)} %param.20) | copy-start | bytes 12292
  6.5 148.7 %all-gather.7.cloned.1.call-start = ((), (), s32[]{:S(2)}) async-start(), calls=%async_computation.3 | async-start | bytes 17301504 | tf_op jit(solution)/shard_map/all_gather | solution.py:14
  12.6 292.8 %all-gather.5.cloned.1.call-start = ((), (), s32[]{:S(2)}) async-start(), calls=%async_computation.1 | async-start | bytes 17301504 | tf_op jit(solution)/shard_map/all_gather | solution.py:110
  13.4 341.3 %reduce-scatter.2.cloned.1.call-start = ((), (), s32[]{:S(2)}) async-start(), calls=%async_computation.2 | async-start | bytes 4718592 | tf_op jit(solution)/shard_map/reduce_scatter | solution.py:112
Sparse Core Ops, SparseCore 0:
  12.7 142.4 all-gather.6
  157.7 147.7 all-gather.4
  315.8 38.8 reduce-scatter.1
where the time goes:
time: 365 us; the launch traced here: 363 us
  waiting for transfers between devices  210 us (58%)
  blocking collectives  74.4 us (20%)
  other arithmetic  43.9 us (12%)
  matrix products  16.4 us (4%)
  between operations  13.9 us (4%)
    all_gather x1, waiting for transfers between devices, shards(): lax.all_gather(w_out, 'seq', axis=1, tiled=True)  109 us
    unnamed x1, blocking collectives  74.4 us
    all_gather x1, waiting for transfers between devices, prefix(): everything = jax.tree.map(lambda part: lax.all_gather(part, axis), array)  61.4 us
    reduce_scatter x1, waiting for transfers between devices, shards(): lax.psum_scatter(partial_out, 'grp', scatter_dimension=1, tiled=True)  39 us
    select_n x32, other arithmetic, turn(): return jax.tree.map(lambda a, b: jnp.where(reached, a, b), new, before)  37.7 us
    dot_general x1, matrix products, shards(): jnp.dot(normed, lax.all_gather(w_out, 'seq', axis=1, tiled=True), preferr...  10.2 us
  transfers between devices with their start and end apart: 3, of which 3 were waited for; matrix products, arithmetic and copies ran while one was open for 13% of the time, Pallas kernels for 0%

commit v1 on v0

--- a/solution.py
+++ b/solution.py
@@ -7,6 +7,11 @@
 CHANNEL_WIDTH = 128
 STATE = 128
 HIGH = lax.Precision.HIGHEST
+
+
+def swapped_in(shard, axis, along):
+    repeated = jnp.stack([shard] * lax.axis_size(axis))
+    return jnp.concatenate(lax.all_to_all(repeated, axis, 0, 0), axis=along)
 
 
 def prefix(array, axis, combine, identity):
@@ -106,9 +111,7 @@
     )
     y = y + skip_d[None, :, None] * xf
     normed = gated_norm_output(y, multiplier_channels, norm_gain, groups)
-    partial_out = jnp.dot(
-        normed, lax.all_gather(w_out, "seq", axis=1, tiled=True), preferred_element_type=jnp.float32
-    )
+    partial_out = jnp.dot(normed, swapped_in(w_out, "seq", 1), preferred_element_type=jnp.float32)
     return lax.psum_scatter(partial_out, "grp", scatter_dimension=1, tiled=True).astype(
         jnp.bfloat16
     )

time: 365 us -> 678 us (1.86)
  blocking collectives: 74.4 us -> 540 us
  waiting for transfers between devices: 210 us -> 37.4 us
  starting transfers between devices: 0.08 us -> 11.9 us
    unnamed x1, blocking collectives: 74.4 us -> 540 us
    all_gather x1 -> x0, waiting for transfers between devices: 109 us -> none  [shards(): lax.all_gather(w_out, 'seq', axis=1, tiled=True)]
    all_gather x1, waiting for transfers between devices: 61.4 us -> 0.02 us  [prefix(): everything = jax.tree.map(lambda part: lax.all_gather(part, axis), array)]
    all_to_all x0 -> x1, starting transfers between devices: none -> 11.9 us  [swapped_in(): return jnp.concatenate(lax.all_to_all(repeated, axis, 0, 0), axis=along)]
  transfers between devices with their start and end apart: 3 -> 3, of which waited for: 3 -> 1; matrix products, arithmetic and copies ran while one was open for 13% -> 7% of each run, Pallas kernels for 0% -> 0%
where the time goes in v1:
time: 678 us; the launch traced here: 676 us
  blocking collectives  540 us (80%)
  other arithmetic  43 us (6%)
  waiting for transfers between devices  37.4 us (6%)
  matrix products  18.2 us (3%)
  between operations  14.3 us (2%)
  starting transfers between devices  11.9 us (2%)
  local copies, waits for them, and re-layouts  10 us (1%)
    unnamed x1, blocking collectives  540 us
    select_n x32, other arithmetic, turn(): return jax.tree.map(lambda a, b: jnp.where(reached, a, b), new, before)  37.6 us
    reduce_scatter x1, waiting for transfers between devices, shards(): lax.psum_scatter(partial_out, 'grp', scatter_dimension=1, tiled=True)  37.4 us
  transfers between devices with their start and end apart: 3, of which 1 were waited for; matrix products, arithmetic and copies ran while one was open for 7% of the time, Pallas kernels for 0%

profile of v1, /device:TPU:8, one launch (start us, length us, event | category | flops | bytes accessed | tf_op | source)
XLA Modules:
  0.0 676.1 jit_solution(8699839942404803319)
XLA Ops:
  6.5 0.7 exponential_negate_fusion
  7.2 0.9 fusion.33
  8.1 0.1 copy.37
  8.2 0.2 reduce_window_sum.13
  8.4 0.8 convert_element_type.21
  9.2 1.1 copy.40
  10.3 0.8 exponential_multiply_fusion
  11.1 1.4 convolution_add_fusion
  12.5 0.0 all-gather.4.cloned.1.call-update
  12.6 1.2 copy.44
  13.8 6.0 stack.2
  19.8 0.0 copy-start
  19.8 0.0 copy-start.3
  19.8 11.9 %all-to-all-start = ((bf16[32,1024,256]{1,2,0:T(8,128)(2,1)}), bf16[32,1024,256]{1,2,0:T(8,128)(2,1)}, u32[]{:S(2)}, u32[]{:S(2)}) async-start(bf16[32,1024,256]{1,2,0:T(8,128)(2,1)} %stack.2), calls=%async_computation | async-start | bytes 33554432 | tf_op jit(solution)/shard_map/all_to_all | solution.py:14
  31.8 0.0 reduce-scatter.2.cloned.1.call-start
  31.9 0.7 dynamic-slice.6
  33.2 0.1 exponential_dynamic-update-slice_fusion
  33.3 540.2 %all-reduce = f32[256]{0:T(256)S(1)} all-reduce(f32[256]{0:T(256)S(1)} %exponential_dynamic-update-slice_fusion), channel_id=2, replica_groups=mesh['seq'=32,'grp'=8] {'seq'}, use_global_device_ids=true, to_apply=%add | all-reduce | flops 256 | bytes 2048
  573.6 0.1 reshape.124
  573.7 0.1 copy.41
  573.8 0.1 fusion.34
  574.0 0.8 convolution_bitcast_fusion
  574.8 1.2 fusion.5
  576.0 0.0 all-gather.4.cloned.1.call-done
  576.0 39.0 %while.9 = (s32[]{:T(128)}, f32[8,128,128]{2,1,0:T(8,128)S(1)}, s32[]{:T(128)}, f32[32,8]{1,0:T(8,128)S(1)}, f32[32,8,128,128]{3,2,1,0:T(8,128)}, /*index=5*/s32[]{:T(128)}, s32[]{:T(128)}) while((s32[]{:T(128)}, f32[8,128,128]{2,1,0:T(8,128)S(1)}, s32[]{:T(128)}, f32[32,8]{1,0:T(8,128)S(1)}, f32[32,8,128,128]{3,2,1,0:T(8,128)}, ...), condition=%wide.region_3.4_spmd.clone, body=%wide.region_2.3_spmd.clone.sunk | while | flops 524292 | bytes 1573073 | solution.py:31
  576.0 1.2 fusion.41
  577.3 1.2 fusion.41
  578.5 1.2 fusion.41
  579.7 1.2 fusion.41
  580.9 1.2 fusion.41
  582.1 1.2 fusion.41
  583.3 1.2 fusion.41
  584.6 1.2 fusion.41
  585.8 1.2 fusion.41
  587.0 1.2 fusion.41
  588.2 1.2 fusion.41
  589.4 1.2 fusion.41
  590.7 1.2 fusion.41
  591.9 1.2 fusion.41
  593.1 1.2 fusion.41
  594.3 1.2 fusion.41
  595.5 1.2 fusion.41
  596.7 1.2 fusion.41
  598.0 1.2 fusion.41
  599.2 1.2 fusion.41
  600.4 1.2 fusion.41
  601.6 1.2 fusion.41
  602.8 1.2 fusion.41
  604.1 1.2 fusion.41
  605.3 1.2 fusion.41
  606.5 1.2 fusion.41
  607.7 1.2 fusion.41
  608.9 1.2 fusion.41
  610.1 1.2 fusion.41
  611.4 1.2 fusion.41
  612.6 1.2 fusion.41
  613.8 1.2 fusion.41
  615.0 1.2 fusion.3
  616.2 0.2 copy.43
  616.4 0.2 multiply_reduce_fusion
  616.7 13.4 %fusion.15 = f32[128,8192]{1,0:T(8,128)} fusion(bf16[1024,8192]{0,1:T(8,128)(2,1)} %bitcast.11, f32[1024]{0:T(1024)S(1)} %copy-done.3, f32[128]{0:T(128)S(1)} %add_rsqrt_fusion, f32[128,1024]{1,0:T(8,128)S(1)} %copy.43, bf16[128,1024]{1,0:T(8,128)(2,1)S(1)} %copy-done), kind=kOutput, calls=%fused_computation.27 | convolution fusion | flops 2148663296 | bytes 21762560 | tf_op jit(solution)/shard_map/dot_general | solution.py:114
  630.1 0.0 reduce-scatter.2.cloned.1.call-update
  630.1 37.4 %reduce-scatter.2.cloned.1.call-done = f32[128,1024]{1,0:T(8,128)} async-done(((f32[128,8192]{1,0:T(8,128)}), f32[128,1024]{1,0:T(8,128)}) %reduce-scatter.2.cloned.1.call-update) | async-done | bytes 524304 | tf_op jit(solution)/shard_map/reduce_scatter | solution.py:115
  667.5 1.8 convert_element_type.24
  (54 shorter events, 0.5 us)
Async XLA Ops:
  6.5 569.5 %all-gather.4.cloned.1.call-start = ((), (), s32[]{:S(2)}) async-start(), calls=%async_computation.3 | async-start | bytes 17301504 | tf_op jit(solution)/shard_map/all_gather | solution.py:19
  19.8 12.0 %copy-start.5 = (u32[256]{0:T(256)S(1)}, u32[256]{0:T(256)}, u32[]{:S(2)}) copy-start(u32[256]{0:T(256)} %constant.71) | copy-start | bytes 3076
  19.8 553.8 %copy-start.2 = (bf16[128,128]{1,0:T(8,128)(2,1)S(1)}, bf16[128,128]{1,0:T(8,128)(2,1)}, u32[]{:S(2)}) copy-start(bf16[128,128]{1,0:T(8,128)(2,1)} %param.15) | copy-start | bytes 98308
  19.8 554.0 %copy-start.1 = (bf16[128,128]{1,0:T(8,128)(2,1)S(1)}, bf16[128,128]{1,0:T(8,128)(2,1)}, u32[]{:S(2)}) copy-start(bf16[128,128]{1,0:T(8,128)(2,1)} %param.14) | copy-start | bytes 98308
  19.8 595.2 %copy-start.4 = (f32[8]{0:T(128)S(1)}, f32[8]{0:T(128)}, u32[]{:S(2)}) copy-start(f32[8]{0:T(128)} %param.19) | copy-start | bytes 100
  19.8 596.6 %copy-start = (bf16[128,1024]{1,0:T(8,128)(2,1)S(1)}, bf16[128,1024]{1,0:T(8,128)(2,1)}, u32[]{:S(2)}) copy-start(bf16[128,1024]{1,0:T(8,128)(2,1)} %param.13) | copy-start | bytes 786436
  19.8 596.8 %copy-start.3 = (f32[1024]{0:T(1024)S(1)}, f32[1024]{0:T(1024)}, u32[]{:S(2)}) copy-start(f32[1024]{0:T(1024)} %param.20) | copy-start | bytes 12292
  19.8 596.8 %all-to-all-start = ((bf16[32,1024,256]{1,2,0:T(8,128)(2,1)}), bf16[32,1024,256]{1,2,0:T(8,128)(2,1)}, u32[]{:S(2)}, u32[]{:S(2)}) async-start(bf16[32,1024,256]{1,2,0:T(8,128)(2,1)} %stack.2), calls=%async_computation | async-start | bytes 33554432 | tf_op jit(solution)/shard_map/all_to_all | solution.py:14
  31.8 635.7 %reduce-scatter.2.cloned.1.call-start = ((), (), s32[]{:S(2)}) async-start(), calls=%async_computation.2 | async-start | bytes 4718592 | tf_op jit(solution)/shard_map/reduce_scatter | solution.py:115
Sparse Core Ops, SparseCore 0:
  12.7 432.0 all-gather.3
  630.2 37.2 reduce-scatter.1
